TPU v7x, 256 devices: a whole 4x4x8 slice. The times are simulated.
256 devices in a mesh: own: 2 (over y_hi), space: 128 (over z, x, y_lo, core).
Axes of the slice: x: 4, y: 4 (y_hi: 2, y_lo: 2; y = y_hi * 2 + y_lo), z: 8, core: 2. Of those that a mesh axis runs over, the one named last changes fastest.
Arguments:
- density: bfloat16 [256, 4, 512, 128], P(None, 'own', 'space'), may hold values from -6 to 6
- cotangent: bfloat16 [256, 4, 512, 128], P(None, 'own', 'space'), may hold values from -6 to 6
- pw_one: bfloat16 [256, 256], P('own'), may hold values from -0.375 to 0.375
- pw_two: bfloat16 [256, 256], P('own'), may hold values from -0.375 to 0.375
- dw_one: bfloat16 [27, 256], P(None, 'own'), may hold values from -1.25 to 1.25
- dw_two: bfloat16 [27, 256], P(None, 'own'), may hold values from -1.25 to 1.25
Outputs:
- grad_input: bfloat16 [256, 4, 512, 128], P(None, 'own', 'space')
- grad_pw_one: float32 [256, 256], P('own')
- grad_pw_two: float32 [256, 256], P('own')
- grad_dw_one: float32 [27, 256], P(None, 'own')
- grad_dw_two: float32 [27, 256], P(None, 'own')
All inputs are finite; a program needn't handle non-finite values.
Results may differ from a plain program's by a relative error of at most 0.01.
Values may be sent and summed in bfloat16 or wider, within the bound.
A program may use at most 192 MiB of HBM per device.

v0:
```python
import math
import jax
import jax.numpy as jnp
from jax import lax
from jax.sharding import PartitionSpec as P

TAP_LIST = [
    (9 * (a + 1) + 3 * (b + 1) + (d + 1), a, b, d)
    for a in (-1, 0, 1)
    for b in (-1, 0, 1)
    for d in (-1, 0, 1)
]


def extended(value, sides, width):
    for axis, dim in sides:
        size, length = (lax.axis_size(axis), value.shape[dim])
        up = [(i, (i + 1) % size) for i in range(size)]
        down = [(j, i) for i, j in up]
        last = lax.slice_in_dim(value, length - width, length, axis=dim)
        first = lax.slice_in_dim(value, 0, width, axis=dim)
        before = lax.ppermute(last, axis, up)
        after = lax.ppermute(first, axis, down)
        value = jnp.concatenate([before, value, after], axis=dim)
    return value


def depthwise(padded, weights, extent_x, extent_y, direction):
    running = jnp.zeros((padded.shape[0], extent_x, extent_y, padded.shape[3]), jnp.float32)
    for k, a, b, d in TAP_LIST:
        start_x = 1 + direction * a
        start_y = 1 + direction * b
        shifted = padded[:, start_x : start_x + extent_x, start_y : start_y + extent_y, :]
        shifted = jnp.roll(shifted, -direction * d, axis=3).astype(jnp.float32)
        running = running + weights[k].astype(jnp.float32)[:, None, None, None] * shifted
    return running


def tap_sums(padded, gradient):
    extent_x = gradient.shape[1]
    extent_y = gradient.shape[2]
    grad_float = gradient.astype(jnp.float32)
    columns = []
    for k, a, b, d in TAP_LIST:
        shifted = padded[:, 1 + a : 1 + a + extent_x, 1 + b : 1 + b + extent_y, :]
        shifted = jnp.roll(shifted, -d, axis=3).astype(jnp.float32)
        columns.append(jnp.sum(shifted * grad_float, axis=(1, 2, 3)))
    return jnp.stack(columns, axis=0)


def pointwise(weights, source):
    layout = source.shape
    flattened = source.reshape(layout[0], -1)
    return jnp.dot(weights.T, flattened, preferred_element_type=jnp.float32).reshape(layout)


def backmap(weights, source):
    layout = source.shape
    flattened = source.reshape(layout[0], -1)
    return jnp.dot(weights, flattened, preferred_element_type=jnp.float32).reshape(layout)


def contract_cells(left, right):
    channels = left.shape[0]
    return lax.dot_general(
        left.reshape(channels, -1),
        right.reshape(channels, -1),
        (((1,), (1,)), ((), ())),
        preferred_element_type=jnp.float32,
    )


def shards(density, cotangent, pw_one, pw_two, dw_one, dw_two):
    channels, extent_x, extent_y, extent_z = density.shape
    weight_one, weight_two, taps_one, taps_two = (
        lax.all_gather(pw_one, "own", axis=0, tiled=True),
        lax.all_gather(pw_two, "own", axis=0, tiled=True),
        lax.all_gather(dw_one, "own", axis=1, tiled=True),
        lax.all_gather(dw_two, "own", axis=1, tiled=True),
    )
    rim_width = 1
    wide_input = extended(density, (("own", 1), ("space", 2)), rim_width)
    first = depthwise(wide_input, taps_one, extent_x, extent_y, 1).astype(jnp.bfloat16)
    pre = pointwise(weight_one, first)
    act = jax.nn.silu(pre).astype(jnp.bfloat16)
    act_padded = extended(act, (("own", 1), ("space", 2)), 1)
    second = depthwise(act_padded, taps_two, extent_x, extent_y, 1).astype(jnp.bfloat16)
    grad_second = backmap(weight_two, cotangent).astype(jnp.bfloat16)
    second_padded = extended(grad_second, (("own", 1), ("space", 2)), 1)
    sigma = jax.nn.sigmoid(pre)
    grad_pre = (
        depthwise(second_padded, taps_two, extent_x, extent_y, -1)
        * (sigma * (1.0 + pre * (1.0 - sigma)))
    ).astype(jnp.bfloat16)
    grad_first = backmap(weight_one, grad_pre).astype(jnp.bfloat16)
    first_padded = extended(grad_first, (("own", 1), ("space", 2)), 1)
    grad_input = (
        cotangent.astype(jnp.float32) + depthwise(first_padded, taps_one, extent_x, extent_y, -1)
    ).astype(jnp.bfloat16)
    total_cells = extent_x * extent_y * extent_z * lax.axis_size("own") * lax.axis_size("space")
    grad_scale = 1.0 / math.sqrt(float(total_cells))
    local_pw_one = contract_cells(first, grad_pre) * grad_scale
    local_pw_two = contract_cells(second, cotangent) * grad_scale
    local_dw_one = tap_sums(wide_input, grad_first) * grad_scale
    local_dw_two = tap_sums(act_padded, grad_second) * grad_scale
    partials = (local_pw_one, local_pw_two, local_dw_one, local_dw_two)
    summed = lax.psum((partials[0], partials[1], partials[2], partials[3]), ("own", "space"))
    share_rows = channels // lax.axis_size("own")
    position = lax.axis_index("own") * share_rows
    result = (
        lax.dynamic_slice_in_dim(summed[0], position, share_rows, 0),
        lax.dynamic_slice_in_dim(summed[1], position, share_rows, 0),
        lax.dynamic_slice_in_dim(summed[2], position, share_rows, 1),
        lax.dynamic_slice_in_dim(summed[3], position, share_rows, 1),
    )
    return (grad_input, result[0], result[1], result[2], result[3])


def solution(mesh):
    in_specs = (
        P(None, "own", "space", None),
        P(None, "own", "space", None),
        P("own", None),
        P("own", None),
        P(None, "own"),
        P(None, "own"),
    )
    out_specs = (
        P(None, "own", "space", None),
        P("own", None),
        P("own", None),
        P(None, "own"),
        P(None, "own"),
    )
    return jax.shard_map(shards, mesh=mesh, in_specs=in_specs, out_specs=out_specs, check_vma=False)
```

profile of v0, /device:TPU:1, one launch (start us, length us, event | category | flops | bytes accessed | tf_op | source)
XLA Modules:
  0.0 458.6 jit_solution(16944286519748687142)
XLA Ops:
  8.7 3.8 collective-permute-start.5
  12.6 11.0 %all_gather.12 = bf16[27,256]{1,0:T(8,128)(2,1)S(1)} all-gather(bf16[27,128]{1,0:T(8,128)(2,1)S(1)} %copy-done.80), channel_id=1, replica_groups=mesh['own'=2,'space'=128] {'own'}, dimensions={1}, use_global_device_ids=true | all-gather | bytes 20736 | tf_op jit(solution)/shard_map/all_gather | solution.py:78
  24.9 5.3 %all_gather.13 = bf16[27,256]{1,0:T(8,128)(2,1)S(1)} all-gather(bf16[27,128]{1,0:T(8,128)(2,1)S(1)} %copy-done.81), channel_id=1, replica_groups=mesh['own'=2,'space'=128] {'own'}, dimensions={1}, use_global_device_ids=true | all-gather | bytes 20736 | tf_op jit(solution)/shard_map/all_gather | solution.py:79
  31.5 5.3 %all_gather.15 = bf16[256,256]{1,0:T(8,128)(2,1)S(1)} all-gather(bf16[128,256]{1,0:T(8,128)(2,1)S(1)} %copy-done.24), channel_id=1, replica_groups=mesh['own'=2,'space'=128] {'own'}, dimensions={0}, use_global_device_ids=true | all-gather | bytes 196608 | tf_op jit(solution)/shard_map/all_gather | solution.py:76
  39.3 5.4 %all_gather.14 = bf16[256,256]{1,0:T(8,128)(2,1)} all-gather(bf16[128,256]{1,0:T(8,128)(2,1)S(1)} %copy-done.25), channel_id=1, replica_groups=mesh['own'=2,'space'=128] {'own'}, dimensions={0}, use_global_device_ids=true | all-gather | bytes 196608 | tf_op jit(solution)/shard_map/all_gather | solution.py:77
  45.0 6.1 %collective-permute-start.6 = (bf16[256,4,1,128]{3,0,2,1:T(8,128)(2,1)S(1)}, bf16[256,4,1,128]{3,0,2,1:T(8,128)(2,1)}, u32[]{:S(2)}, u32[]{:S(2)}) collective-permute-start(bf16[256,4,1,128]{3,0,2,1:T(8,128)(2,1)S(1)} %copy.93), channel_id=1, source_target_pairs={{0,1},{1,2},{2,3},{3,4},{4,5},{5,6},{6,7},{7,8},{8,9},{9,10},{10,1... | collective-permute-start | bytes 786440 | tf_op jit(solution)/shard_map/ppermute | solution.py:22
  57.6 3.4 collective-permute-done.7
  66.4 11.0 %add_convert_fusion = (bf16[256,2,4,128]{0,3,2,1:T(8,128)(2,1)S(1)}, f32[256,2,4,128]{0,3,2,1:T(8,128)}, f32[256,2,4,128]{0,3,2,1:T(8,128)}, f32[256,2,4,128]{0,...) fusion(bf16[256,2,4,128]{0,3,2,1:T(8,128)(2,1)S(1)} %copy.90, ...), kind=kLoop, calls=%fused_computation.272 | loop fusion | flops 57933824 | bytes 27225088 | tf_op jit(solution)/shard_map/convert_element_type | solution.py:83
  78.7 2.6 collective-permute-start.13
  83.7 2.8 collective-permute-done.13
  86.5 5.6 %collective-permute-done.12 = bf16[256,1,4,128]{0,3,2,1:T(8,128)(2,1)S(1)} collective-permute-done((bf16[256,1,4,128]{0,3,2,1:T(8,128)(2,1)S(1)}, bf16[256,1,4,128]{0,3,2,1:T(8,128)(2,1)S(1)}, u32[]{:S(2)}, u32[]{:S(2)}) %collective-permute-start.12) | collective-permute-done | bytes 262176 | tf_op jit(solution)/shard_map/ppermute | solution.py:22
  103.8 2.9 collective-permute-start
  112.7 5.8 %fusion = f32[256,256]{1,0:T(8,128)} fusion(bf16[256,2,4,128]{0,3,2,1:T(8,128)(2,1)S(1)} %copy-done.11, bf16[256,2,4,128]{0,3,2,1:T(8,128)(2,1)S(1)} %multiply_convert_fusion, f32[256]{0:T(256)S(1)} %bitcast.317, f32[256]{0:T(256)S(1)} %bitcast.319, f32[256]{0:T(256)S(1)} %bitcast.321, f32[256]{0:T(256)S(1)} %bitcast.323, f32[256]{0:T(256)S(1)} %bitcast.325, ...), kind=kOutput, calls=%fused_computation.119 | convolution fusion | flops 192217088 | bytes 14986240 | tf_op jit(solution)/shard_map/dot_general | solution.py:65
  119.7 5.2 %stack.223 = f32[27,256]{1,0:T(8,128)} concatenate(f32[1,256]{1,0:T(1,128)} %bitcast.379, f32[1,256]{1,0:T(1,128)} %bitcast.306, f32[1,256]{1,0:T(1,128)} %bitcast.380, f32[1,256]{1,0:T(1,128)} %bitcast.309, f32[1,256]{1,0:T(1,128)} %bitcast.381, f32[1,256]{1,0:T(1,128)} %bitcast.310, f32[1,256]{1,0:T(1,128)S(1)} %bitcast.275, f32[1,256]{1,0:T(1,128)} %bitcast.303, ...), dimensions={0} | concatenate | bytes 55296 | tf_op jit(solution)/shard_map/stack | solution.py:48
  126.4 3.4 collective-permute-start.3
  132.9 3.0 collective-permute-done.3
  138.4 9.1 %fusion.139 = bf16[256,2,4,128]{0,3,2,1:T(8,128)(2,1)S(1)} fusion(f32[256,2,4,128]{0,3,2,1:T(8,128)S(1)} %bitcast.215, bf16[256,2,4,128]{0,3,2,1:T(8,128)(2,1)S(1)} %get-tuple-element.274, bf16[256,1,4,128]{0,3,2,1:T(8,128)(2,1)S(1)} %collective-permute-done, bf16[256,1,4,128]{0,3,2,1:T(8,128)(2,1)S(1)} %collective-permute-done.1, ...), kind=kLoop, calls=%fused_computation.274 | loop fusion | flops 58982400 | bytes 14666752 | tf_op jit(solution)/shard_map/convert_element_type | solution.py:94
  149.4 8.2 %fusion.95 = (f32[256]{0:T(256)S(1)}, f32[256]{0:T(256)S(1)}, f32[256]{0:T(256)S(1)}, f32[256]{0:T(256)S(1)}, f32[256]{0:T(256)}, /*index=5*/f32[256]{0:T(256)},...) fusion(f32[256,2,4,128]{0,3,2,1:T(8,128)} %get-tuple-element.96, ...), kind=kOutput, calls=%fused_computation.227 | convolution fusion | flops 144174592 | bytes 20072448 | tf_op jit(solution)/shard_map/dot_general | solution.py:60
  158.4 2.9 collective-permute-start.8
  164.1 87.9 %all-reduce = (f32[27,256]{1,0:T(8,128)S(1)}, f32[27,256]{1,0:T(8,128)S(1)}) all-reduce(f32[27,256]{1,0:T(8,128)S(1)} %broadcast_multiply_fusion.1, f32[27,256]{1,0:T(8,128)S(1)} %copy-done.23), channel_id=1, replica_groups=mesh['own'=2,'space'=128] {'own','space'}, use_global_device_ids=true, to_apply=%region_29.30 | all-reduce | flops 13824 | bytes 110592 | tf_op jit(solution)/shard_map/psum | solution.py:107
  253.2 168.2 %all-reduce.4.cloned.1.call-done = (f32[256,256]{1,0:T(8,128)}, f32[256,256]{1,0:T(8,128)}) async-done(((f32[256,256]{1,0:T(8,128)}, f32[256,256]{1,0:T(8,128)}), (f32[256,256]{1,0:T(8,128)}, f32[256,256]{1,0:T(8,128)})) %all-reduce.4.cloned.1.call-update) | async-done | bytes 524304 | tf_op jit(solution)/shard_map/psum | solution.py:107
  424.8 3.3 collective-permute-start.11
  431.5 5.6 %collective-permute-done.10 = bf16[256,4,1,128]{3,0,2,1:T(8,128)(2,1)S(1)} collective-permute-done((bf16[256,4,1,128]{3,0,2,1:T(8,128)(2,1)S(1)}, bf16[256,4,1,128]{3,0,2,1:T(8,128)(2,1)S(1)}, u32[]{:S(2)}, u32[]{:S(2)}) %collective-permute-start.10) | collective-permute-done | bytes 262176 | tf_op jit(solution)/shard_map/ppermute | solution.py:23
  440.0 9.5 %fusion.138 = bf16[256,2,4,128]{0,3,2,1:T(8,128)(2,1)} fusion(bf16[256,2,4,128]{0,3,2,1:T(8,128)(2,1)S(1)} %bitcast.213, bf16[256,2,4,128]{0,3,2,1:T(8,128)(2,1)S(1)} %copy-done.12, bf16[256,1,4,128]{0,3,2,1:T(8,128)(2,1)S(1)} %collective-permute-done.8, bf16[256,1,4,128]{0,3,2,1:T(8,128)(2,1)S(1)} %collective-permute-done.9, ...), kind=kLoop, calls=%fused_computation.273 | loop fusion | flops 57409536 | bytes 14142464 | tf_op jit(solution)/shard_map/convert_element_type | solution.py:99
  (384 shorter events, 64.6 us)
Async XLA Ops:
  7.2 5.4 %copy-start.80 = (bf16[27,128]{1,0:T(8,128)(2,1)S(1)}, bf16[27,128]{1,0:T(8,128)(2,1)}, u32[]{:S(2)}) copy-start(bf16[27,128]{1,0:T(8,128)(2,1)} %param.10) | copy-start | bytes 20740
  7.2 17.7 %copy-start.81 = (bf16[27,128]{1,0:T(8,128)(2,1)S(1)}, bf16[27,128]{1,0:T(8,128)(2,1)}, u32[]{:S(2)}) copy-start(bf16[27,128]{1,0:T(8,128)(2,1)} %param.11) | copy-start | bytes 20740
  7.2 24.3 %copy-start.24 = (bf16[128,256]{1,0:T(8,128)(2,1)S(1)}, bf16[128,256]{1,0:T(8,128)(2,1)}, u32[]{:S(2)}) copy-start(bf16[128,256]{1,0:T(8,128)(2,1)} %param.8) | copy-start | bytes 196612
  7.2 29.6 %copy-start.18 = (bf16[256,2,4,128]{3,2,1,0:T(4,128)(2,1)S(1)}, bf16[256,2,4,128]{3,2,1,0:T(4,128)(2,1)}, u32[]{:S(2)}) copy-start(bf16[256,2,4,128]{3,2,1,0:T(4,128)(2,1)} %param.7) | copy-start | bytes 1572868
  7.2 414.2 %all-reduce.4.cloned.1.call-start = ((), (), s32[]{:S(2)}) async-start(), calls=%async_computation | async-start | bytes 1048576 | tf_op jit(solution)/shard_map/psum | solution.py:107
  8.7 36.1 %collective-permute-start.5 = (bf16[256,1,4,128]{0,3,2,1:T(8,128)(2,1)S(1)}, bf16[256,1,4,128]{0,3,2,1:T(8,128)(2,1)S(1)}, u32[]{:S(2)}, u32[]{:S(2)}) collective-permute-start(bf16[256,1,4,128]{0,3,2,1:T(8,128)(2,1)S(1)} %get-tuple-element.218), channel_id=1, source_target_pairs={{128,0},{0,128},{129,1},{1,129},{130,2},{2,130},{131,3},{3,131},{1... | collective-permute-start | bytes 786440 | tf_op jit(solution)/shard_map/ppermute | solution.py:23
  12.5 32.3 %collective-permute-start.4 = (bf16[256,1,4,128]{0,3,2,1:T(8,128)(2,1)S(1)}, bf16[256,1,4,128]{0,3,2,1:T(8,128)(2,1)S(1)}, u32[]{:S(2)}, u32[]{:S(2)}) collective-permute-start(bf16[256,1,4,128]{0,3,2,1:T(8,128)(2,1)S(1)} %get-tuple-element.217), channel_id=1, source_target_pairs={{0,128},{128,0},{1,129},{129,1},{2,130},{130,2},{3,131},{131,3},{4... | collective-permute-start | bytes 786440 | tf_op jit(solution)/shard_map/ppermute | solution.py:22
  45.0 10.7 %collective-permute-start.6 = (bf16[256,4,1,128]{3,0,2,1:T(8,128)(2,1)S(1)}, bf16[256,4,1,128]{3,0,2,1:T(8,128)(2,1)}, u32[]{:S(2)}, u32[]{:S(2)}) collective-permute-start(bf16[256,4,1,128]{3,0,2,1:T(8,128)(2,1)S(1)} %copy.93), channel_id=1, source_target_pairs={{0,1},{1,2},{2,3},{3,4},{4,5},{5,6},{6,7},{7,8},{8,9},{9,10},{10,1... | collective-permute-start | bytes 786440 | tf_op jit(solution)/shard_map/ppermute | solution.py:22
  52.0 8.9 %collective-permute-start.7 = (bf16[256,4,1,128]{3,0,2,1:T(8,128)(2,1)}, bf16[256,4,1,128]{3,0,2,1:T(8,128)(2,1)}, u32[]{:S(2)}, u32[]{:S(2)}) collective-permute-start(bf16[256,4,1,128]{3,0,2,1:T(8,128)(2,1)} %copy.96), channel_id=1, source_target_pairs={{1,0},{2,1},{3,2},{4,3},{5,4},{6,5},{7,6},{8,7},{9,8},{10,9},{11,1... | collective-permute-start | bytes 786440 | tf_op jit(solution)/shard_map/ppermute | solution.py:23
  78.7 7.8 %collective-permute-start.13 = (bf16[256,1,4,128]{0,3,2,1:T(8,128)(2,1)S(1)}, bf16[256,1,4,128]{0,3,2,1:T(8,128)(2,1)S(1)}, u32[]{:S(2)}, u32[]{:S(2)}) collective-permute-start(bf16[256,1,4,128]{0,3,2,1:T(8,128)(2,1)S(1)} %get-tuple-element.190), channel_id=1, source_target_pairs={{128,0},{0,128},{129,1},{1,129},{130,2},{2,130},{131,3},{3,131},{1... | collective-permute-start | bytes 786440 | tf_op jit(solution)/shard_map/ppermute | solution.py:23
  81.3 10.8 %collective-permute-start.12 = (bf16[256,1,4,128]{0,3,2,1:T(8,128)(2,1)S(1)}, bf16[256,1,4,128]{0,3,2,1:T(8,128)(2,1)S(1)}, u32[]{:S(2)}, u32[]{:S(2)}) collective-permute-start(bf16[256,1,4,128]{0,3,2,1:T(8,128)(2,1)S(1)} %get-tuple-element.189), channel_id=1, source_target_pairs={{0,128},{128,0},{1,129},{129,1},{2,130},{130,2},{3,131},{131,3},{4... | collective-permute-start | bytes 786440 | tf_op jit(solution)/shard_map/ppermute | solution.py:22
  92.2 4.9 %collective-permute-start.14 = (bf16[256,4,1,128]{0,3,2,1:T(8,128)(2,1)S(1)}, bf16[256,4,1,128]{0,3,2,1:T(8,128)(2,1)S(1)}, u32[]{:S(2)}, u32[]{:S(2)}) collective-permute-start(bf16[256,4,1,128]{0,3,2,1:T(8,128)(2,1)S(1)} %get-tuple-element.147), channel_id=1, source_target_pairs={{0,1},{1,2},{2,3},{3,4},{4,5},{5,6},{6,7},{7,8},{8,9},{9,10},{10,1... | collective-permute-start | bytes 786440 | tf_op jit(solution)/shard_map/ppermute | solution.py:22
  93.7 5.8 %collective-permute-start.15 = (bf16[256,4,1,128]{0,3,2,1:T(8,128)(2,1)S(1)}, bf16[256,4,1,128]{0,3,2,1:T(8,128)(2,1)S(1)}, u32[]{:S(2)}, u32[]{:S(2)}) collective-permute-start(bf16[256,4,1,128]{0,3,2,1:T(8,128)(2,1)S(1)} %get-tuple-element.148), channel_id=1, source_target_pairs={{1,0},{2,1},{3,2},{4,3},{5,4},{6,5},{7,6},{8,7},{9,8},{10,9},{11,1... | collective-permute-start | bytes 786440 | tf_op jit(solution)/shard_map/ppermute | solution.py:23
  103.8 22.5 %collective-permute-start = (bf16[256,1,4,128]{0,3,2,1:T(8,128)(2,1)}, bf16[256,1,4,128]{0,3,2,1:T(8,128)(2,1)S(1)}, u32[]{:S(2)}, u32[]{:S(2)}) collective-permute-start(bf16[256,1,4,128]{0,3,2,1:T(8,128)(2,1)} %get-tuple-element.210), channel_id=1, source_target_pairs={{0,128},{128,0},{1,129},{129,1},{2,130},{130,2},{3,131},{131,3},{4... | collective-permute-start | bytes 786440 | tf_op jit(solution)/shard_map/ppermute | solution.py:22
  106.7 19.6 %collective-permute-start.1 = (bf16[256,1,4,128]{0,3,2,1:T(8,128)(2,1)}, bf16[256,1,4,128]{0,3,2,1:T(8,128)(2,1)S(1)}, u32[]{:S(2)}, u32[]{:S(2)}) collective-permute-start(bf16[256,1,4,128]{0,3,2,1:T(8,128)(2,1)} %get-tuple-element.209), channel_id=1, source_target_pairs={{128,0},{0,128},{129,1},{1,129},{130,2},{2,130},{131,3},{3,131},{1... | collective-permute-start | bytes 786440 | tf_op jit(solution)/shard_map/ppermute | solution.py:23
  126.4 9.6 %collective-permute-start.3 = (bf16[256,4,1,128]{0,3,2,1:T(8,128)(2,1)S(1)}, bf16[256,4,1,128]{0,3,2,1:T(8,128)(2,1)S(1)}, u32[]{:S(2)}, u32[]{:S(2)}) collective-permute-start(bf16[256,4,1,128]{0,3,2,1:T(8,128)(2,1)S(1)} %get-tuple-element.156), channel_id=1, source_target_pairs={{0,1},{1,2},{2,3},{3,4},{4,5},{5,6},{6,7},{7,8},{8,9},{9,10},{10,1... | collective-permute-start | bytes 786440 | tf_op jit(solution)/shard_map/ppermute | solution.py:22
  129.8 6.1 %collective-permute-start.2 = (bf16[256,4,1,128]{0,3,2,1:T(8,128)(2,1)S(1)}, bf16[256,4,1,128]{0,3,2,1:T(8,128)(2,1)S(1)}, u32[]{:S(2)}, u32[]{:S(2)}) collective-permute-start(bf16[256,4,1,128]{0,3,2,1:T(8,128)(2,1)S(1)} %get-tuple-element.155), channel_id=1, source_target_pairs={{1,0},{2,1},{3,2},{4,3},{5,4},{6,5},{7,6},{8,7},{9,8},{10,9},{11,1... | collective-permute-start | bytes 786440 | tf_op jit(solution)/shard_map/ppermute | solution.py:23
  138.4 9.9 %copy-start.20 = (bf16[256,2,4,128]{0,3,2,1:T(8,128)(2,1)S(1)}, bf16[256,2,4,128]{0,3,2,1:T(8,128)(2,1)}, u32[]{:S(2)}) copy-start(bf16[256,2,4,128]{0,3,2,1:T(8,128)(2,1)} %copy-done.19) | copy-start | bytes 1572868
  158.4 266.2 %collective-permute-start.8 = (bf16[256,1,4,128]{0,3,2,1:T(8,128)(2,1)}, bf16[256,1,4,128]{0,3,2,1:T(8,128)(2,1)S(1)}, u32[]{:S(2)}, u32[]{:S(2)}) collective-permute-start(bf16[256,1,4,128]{0,3,2,1:T(8,128)(2,1)} %get-tuple-element.200), channel_id=1, source_target_pairs={{0,128},{128,0},{1,129},{129,1},{2,130},{130,2},{3,131},{131,3},{4... | collective-permute-start | bytes 786440 | tf_op jit(solution)/shard_map/ppermute | solution.py:22
  161.3 263.2 %collective-permute-start.9 = (bf16[256,1,4,128]{0,3,2,1:T(8,128)(2,1)}, bf16[256,1,4,128]{0,3,2,1:T(8,128)(2,1)S(1)}, u32[]{:S(2)}, u32[]{:S(2)}) collective-permute-start(bf16[256,1,4,128]{0,3,2,1:T(8,128)(2,1)} %get-tuple-element.199), channel_id=1, source_target_pairs={{128,0},{0,128},{129,1},{1,129},{130,2},{2,130},{131,3},{3,131},{1... | collective-permute-start | bytes 786440 | tf_op jit(solution)/shard_map/ppermute | solution.py:23
  161.4 2.4 copy-start.82
  161.5 2.5 copy-start.23
  424.8 6.6 %collective-permute-start.11 = (bf16[256,4,1,128]{3,0,2,1:T(8,128)(2,1)S(1)}, bf16[256,4,1,128]{3,0,2,1:T(8,128)(2,1)S(1)}, u32[]{:S(2)}, u32[]{:S(2)}) collective-permute-start(bf16[256,4,1,128]{3,0,2,1:T(8,128)(2,1)S(1)} %copy.106), channel_id=1, source_target_pairs={{0,1},{1,2},{2,3},{3,4},{4,5},{5,6},{6,7},{7,8},{8,9},{9,10},{10,1... | collective-permute-start | bytes 786440 | tf_op jit(solution)/shard_map/ppermute | solution.py:22
  428.2 8.9 %collective-permute-start.10 = (bf16[256,4,1,128]{3,0,2,1:T(8,128)(2,1)S(1)}, bf16[256,4,1,128]{3,0,2,1:T(8,128)(2,1)S(1)}, u32[]{:S(2)}, u32[]{:S(2)}) collective-permute-start(bf16[256,4,1,128]{3,0,2,1:T(8,128)(2,1)S(1)} %copy.104), channel_id=1, source_target_pairs={{1,0},{2,1},{3,2},{4,3},{5,4},{6,5},{7,6},{8,7},{9,8},{10,9},{11,1... | collective-permute-start | bytes 786440 | tf_op jit(solution)/shard_map/ppermute | solution.py:23
  (143 other events, 264.8 us)
Sparse Core Ops, SparseCore 0:
  161.5 259.8 all-reduce.3
where the time goes:
time: 468 us; the launch traced here: 459 us
  waiting for transfers between devices  194 us (41%)
  blocking collectives  115 us (25%)
  other arithmetic  52.1 us (11%)
  local copies, waits for them, and re-layouts  31.8 us (7%)
  starting transfers between devices  31.6 us (7%)
  matrix products  17.5 us (4%)
  between operations  16.6 us (4%)
    psum x1, waiting for transfers between devices, shards(): lax.psum((partials[0], partials[1], partials[2], partials[3]), ('own', 's...  168 us
    psum x1, blocking collectives, shards(): lax.psum((partials[0], partials[1], partials[2], partials[3]), ('own', 's...  87.9 us
    ppermute x8, starting transfers between devices, extended(): before = lax.ppermute(last, axis, up)  21.1 us
    ppermute x8, waiting for transfers between devices, extended(): after = lax.ppermute(first, axis, down)  14.3 us
    ppermute x8, waiting for transfers between devices, extended(): before = lax.ppermute(last, axis, up)  11.7 us
    convert_element_type x1, other arithmetic, shards(): depthwise(wide_input, taps_one, extent_x, extent_y, 1).astype(jnp.bfloat16)  11 us
    all_gather x1, blocking collectives, shards(): lax.all_gather(dw_one, 'own', axis=1, tiled=True)  11 us
    ppermute x8, starting transfers between devices, extended(): after = lax.ppermute(first, axis, down)  10.5 us
  transfers between devices with their start and end apart: 17, of which 9 were waited for; matrix products, arithmetic and copies ran while one was open for 9% of the time, Pallas kernels for 0%

commit v1 on v0

--- a/solution.py
+++ b/solution.py
@@ -104,7 +104,9 @@
     local_dw_one = tap_sums(wide_input, grad_first) * grad_scale
     local_dw_two = tap_sums(act_padded, grad_second) * grad_scale
     partials = (local_pw_one, local_pw_two, local_dw_one, local_dw_two)
-    summed = lax.psum((partials[0], partials[1], partials[2], partials[3]), ("own", "space"))
+    summed = lax.psum(
+        lax.psum((partials[0], partials[1], partials[2], partials[3]), "space"), "own"
+    )
     share_rows = channels // lax.axis_size("own")
     position = lax.axis_index("own") * share_rows
     result = (

time: 468 us -> 1240 us (2.65)
  blocking collectives: 115 us -> 592 us
  waiting for transfers between devices: 194 us -> 472 us
    psum x1 -> x2, blocking collectives: 87.9 us -> 565 us  [the longest x1 554 us: shards(): lax.psum((partials[0], partials[1], partials[2], partials[3]), 'space')]
    psum x1 -> x2, waiting for transfers between devices: 168 us -> 452 us  [the longest x1 421 us: shards(): lax.psum((partials[0], partials[1], partials[2], partials[3]), 'space')]
  transfers between devices with their start and end apart: 17 -> 18, of which waited for: 9 -> 8; matrix products, arithmetic and copies ran while one was open for 9% -> 5% of each run, Pallas kernels for 0% -> 0%
where the time goes in v1:
time: 1240 us; the launch traced here: 1230 us
  blocking collectives  592 us (48%)
  waiting for transfers between devices  472 us (38%)
  other arithmetic  53.8 us (4%)
  starting transfers between devices  39.5 us (3%)
  local copies, waits for them, and re-layouts  35.4 us (3%)
  matrix products  17.5 us (1%)
  between operations  16.5 us (1%)
    psum x1, blocking collectives, shards(): lax.psum((partials[0], partials[1], partials[2], partials[3]), 'space')  554 us
    psum x1, waiting for transfers between devices, shards(): lax.psum((partials[0], partials[1], partials[2], partials[3]), 'space')  421 us
    psum x1, waiting for transfers between devices, shards(): lax.psum(lax.psum((partials[0], partials[1], partials[2], partials[3]), '...  31 us
  transfers between devices with their start and end apart: 18, of which 8 were waited for; matrix products, arithmetic and copies ran while one was open for 5% of the time, Pallas kernels for 0%

profile of v1, /device:TPU:1, one launch (start us, length us, event | category | flops | bytes accessed | tf_op | source)
XLA Modules:
  0.0 1226.2 jit_solution(14830420615026591437)
XLA Ops:
  8.7 3.8 collective-permute-start.5
  12.6 11.0 all_gather.12
  24.9 5.4 all_gather.13
  31.5 5.3 all_gather.15
  39.3 5.4 all_gather.14
  45.0 6.1 collective-permute-start.6
  57.5 3.4 collective-permute-done.7
  66.4 11.0 add_convert_fusion
  83.7 2.9 collective-permute-done.13
  86.5 5.6 collective-permute-done.12
  103.8 2.9 collective-permute-start
  112.7 5.8 fusion
  119.7 5.3 stack.223
  126.4 3.4 collective-permute-start.3
  132.9 3.0 collective-permute-done.3
  138.4 9.1 fusion.139
  149.4 8.3 fusion.95
  158.5 2.9 collective-permute-start.8
  162.9 554.2 %all-reduce = (f32[27,256]{1,0:T(8,128)S(1)}, f32[27,256]{1,0:T(8,128)S(1)}) all-reduce(f32[27,256]{1,0:T(8,128)S(1)} %broadcast_multiply_fusion.1, f32[27,256]{1,0:T(8,128)S(1)} %copy-done.20), channel_id=1, replica_groups=mesh['own'=2,'space'=128] {'space'}, use_global_device_ids=true, to_apply=%region_31.32 | all-reduce | flops 13824 | bytes 110592 | tf_op jit(solution)/shard_map/psum | solution.py:108
  717.0 10.5 all-reduce.2
  731.6 8.9 collective-permute-start.10
  749.7 421.4 %all-reduce.7.cloned.1.call-done = (f32[256,256]{1,0:T(8,128)}, f32[256,256]{1,0:T(8,128)}) async-done(((f32[256,256]{1,0:T(8,128)}, f32[256,256]{1,0:T(8,128)}), (f32[256,256]{1,0:T(8,128)}, f32[256,256]{1,0:T(8,128)})) %all-reduce.7.cloned.1.call-update) | async-done | bytes 524304 | tf_op jit(solution)/shard_map/psum | solution.py:108
  1171.4 11.5 fusion.138
  1185.0 31.0 %all-reduce.9.cloned.1.call-done = (f32[256,256]{1,0:T(8,128)}, f32[256,256]{1,0:T(8,128)}) async-done(((f32[256,256]{1,0:T(8,128)}, f32[256,256]{1,0:T(8,128)}), (f32[256,256]{1,0:T(8,128)}, f32[256,256]{1,0:T(8,128)})) %all-reduce.9.cloned.1.call-update) | async-done | bytes 524304 | tf_op jit(solution)/shard_map/psum | solution.py:107
  (376 shorter events, 71.7 us)
Async XLA Ops:
  7.2 1163.9 %all-reduce.7.cloned.1.call-start = ((), (), s32[]{:S(2)}) async-start(), calls=%async_computation | async-start | bytes 1048576 | tf_op jit(solution)/shard_map/psum | solution.py:108
  8.7 36.1 %collective-permute-start.5 = (bf16[256,1,4,128]{0,3,2,1:T(8,128)(2,1)S(1)}, bf16[256,1,4,128]{0,3,2,1:T(8,128)(2,1)S(1)}, u32[]{:S(2)}, u32[]{:S(2)}) collective-permute-start(bf16[256,1,4,128]{0,3,2,1:T(8,128)(2,1)S(1)} %get-tuple-element.222), channel_id=1, source_target_pairs={{128,0},{0,128},{129,1},{1,129},{130,2},{2,130},{131,3},{3,131},{1... | collective-permute-start | bytes 786440 | tf_op jit(solution)/shard_map/ppermute | solution.py:23
  12.5 32.3 %collective-permute-start.4 = (bf16[256,1,4,128]{0,3,2,1:T(8,128)(2,1)S(1)}, bf16[256,1,4,128]{0,3,2,1:T(8,128)(2,1)S(1)}, u32[]{:S(2)}, u32[]{:S(2)}) collective-permute-start(bf16[256,1,4,128]{0,3,2,1:T(8,128)(2,1)S(1)} %get-tuple-element.221), channel_id=1, source_target_pairs={{0,128},{128,0},{1,129},{129,1},{2,130},{130,2},{3,131},{131,3},{4... | collective-permute-start | bytes 786440 | tf_op jit(solution)/shard_map/ppermute | solution.py:22
  45.0 10.7 collective-permute-start.6
  52.0 8.9 collective-permute-start.7
  78.7 7.8 collective-permute-start.13
  81.3 10.8 collective-permute-start.12
  92.2 4.8 collective-permute-start.14
  93.7 5.8 collective-permute-start.15
  103.8 22.6 %collective-permute-start = (bf16[256,1,4,128]{0,3,2,1:T(8,128)(2,1)}, bf16[256,1,4,128]{0,3,2,1:T(8,128)(2,1)S(1)}, u32[]{:S(2)}, u32[]{:S(2)}) collective-permute-start(bf16[256,1,4,128]{0,3,2,1:T(8,128)(2,1)} %get-tuple-element.214), channel_id=1, source_target_pairs={{0,128},{128,0},{1,129},{129,1},{2,130},{130,2},{3,131},{131,3},{4... | collective-permute-start | bytes 786440 | tf_op jit(solution)/shard_map/ppermute | solution.py:22
  106.7 19.7 %collective-permute-start.1 = (bf16[256,1,4,128]{0,3,2,1:T(8,128)(2,1)}, bf16[256,1,4,128]{0,3,2,1:T(8,128)(2,1)S(1)}, u32[]{:S(2)}, u32[]{:S(2)}) collective-permute-start(bf16[256,1,4,128]{0,3,2,1:T(8,128)(2,1)} %get-tuple-element.213), channel_id=1, source_target_pairs={{128,0},{0,128},{129,1},{1,129},{130,2},{2,130},{131,3},{3,131},{1... | collective-permute-start | bytes 786440 | tf_op jit(solution)/shard_map/ppermute | solution.py:23
  126.4 9.6 collective-permute-start.3
  129.9 6.1 collective-permute-start.2
  158.5 570.4 %collective-permute-start.8 = (bf16[256,1,4,128]{0,3,2,1:T(8,128)(2,1)}, bf16[256,1,4,128]{0,3,2,1:T(8,128)(2,1)S(1)}, u32[]{:S(2)}, u32[]{:S(2)}) collective-permute-start(bf16[256,1,4,128]{0,3,2,1:T(8,128)(2,1)} %get-tuple-element.204), channel_id=1, source_target_pairs={{0,128},{128,0},{1,129},{129,1},{2,130},{130,2},{3,131},{131,3},{4... | collective-permute-start | bytes 786440 | tf_op jit(solution)/shard_map/ppermute | solution.py:22
  161.5 567.3 %collective-permute-start.9 = (bf16[256,1,4,128]{0,3,2,1:T(8,128)(2,1)}, bf16[256,1,4,128]{0,3,2,1:T(8,128)(2,1)S(1)}, u32[]{:S(2)}, u32[]{:S(2)}) collective-permute-start(bf16[256,1,4,128]{0,3,2,1:T(8,128)(2,1)} %get-tuple-element.203), channel_id=1, source_target_pairs={{128,0},{0,128},{129,1},{1,129},{130,2},{2,130},{131,3},{3,131},{1... | collective-permute-start | bytes 786440 | tf_op jit(solution)/shard_map/ppermute | solution.py:23
  162.8 1053.2 %all-reduce.9.cloned.1.call-start = ((), (), s32[]{:S(2)}) async-start(), calls=%async_computation.1 | async-start | bytes 1048576 | tf_op jit(solution)/shard_map/psum | solution.py:107
  729.1 13.2 %collective-permute-start.11 = (bf16[256,4,1,128]{3,0,2,1:T(8,128)(2,1)S(1)}, bf16[256,4,1,128]{3,0,2,1:T(8,128)(2,1)S(1)}, u32[]{:S(2)}, u32[]{:S(2)}) collective-permute-start(bf16[256,4,1,128]{3,0,2,1:T(8,128)(2,1)S(1)} %copy.106), channel_id=1, source_target_pairs={{0,1},{1,2},{2,3},{3,4},{4,5},{5,6},{6,7},{7,8},{8,9},{9,10},{10,1... | collective-permute-start | bytes 786440 | tf_op jit(solution)/shard_map/ppermute | solution.py:22
  731.6 11.4 collective-permute-start.10
  747.4 423.7 %copy-start.32 = (f32[1,256]{1,0:T(1,128)S(1)}, f32[1,256]{1,0:T(1,128)}, u32[]{:S(2)}) copy-start(f32[1,256]{1,0:T(1,128)} %get-tuple-element.254) | copy-start | bytes 3076
  747.4 423.7 %copy-start.34 = (f32[1,256]{1,0:T(1,128)S(1)}, f32[1,256]{1,0:T(1,128)}, u32[]{:S(2)}) copy-start(f32[1,256]{1,0:T(1,128)} %get-tuple-element.255) | copy-start | bytes 3076
  747.4 423.7 %copy-start.36 = (f32[1,256]{1,0:T(1,128)S(1)}, f32[1,256]{1,0:T(1,128)}, u32[]{:S(2)}) copy-start(f32[1,256]{1,0:T(1,128)} %get-tuple-element.256) | copy-start | bytes 3076
  747.4 423.7 %copy-start.38 = (f32[1,256]{1,0:T(1,128)S(1)}, f32[1,256]{1,0:T(1,128)}, u32[]{:S(2)}) copy-start(f32[1,256]{1,0:T(1,128)} %get-tuple-element.257) | copy-start | bytes 3076
  747.5 423.7 %copy-start.40 = (f32[1,256]{1,0:T(1,128)S(1)}, f32[1,256]{1,0:T(1,128)}, u32[]{:S(2)}) copy-start(f32[1,256]{1,0:T(1,128)} %get-tuple-element.258) | copy-start | bytes 3076
  747.5 423.7 %copy-start.42 = (f32[1,256]{1,0:T(1,128)S(1)}, f32[1,256]{1,0:T(1,128)}, u32[]{:S(2)}) copy-start(f32[1,256]{1,0:T(1,128)} %get-tuple-element.259) | copy-start | bytes 3076
  (138 other events, 7940.5 us)
Sparse Core Ops, SparseCore 0:
  162.9 1008.1 all-reduce.6
  1173.9 42.0 all-reduce.8
